TPU v7x, 32 devices: a whole 2x2x4 slice. The times are simulated.
32 devices in a mesh: dp: 2 (over y), ctx: 4 (over x, core), tensor: 4 (over z).
Axes of the slice: x: 2, y: 2, z: 4, core: 2. Of those that a mesh axis runs over, the one named last changes fastest.
Arguments:
- residual: bfloat16 [2048, 3584], P(('dp', 'ctx', 'tensor')), parts along dimension 0, may hold values from -6 to 6
- queries: bfloat16 [2048, 1024], P(('dp', 'ctx'), 'tensor'), parts along dimension 0, may hold values from -8 to 8
- key_heads: bfloat16 [2048, 512], P(('dp', 'ctx'), 'tensor'), parts along dimension 0, may hold values from -8 to 8
- value_heads: bfloat16 [2048, 512], P(('dp', 'ctx'), 'tensor'), parts along dimension 0, may hold values from -6 to 6
- doc_blocks: int32 [12], P('dp'), parts along dimension 0, may hold values from 1 to 16, 32 in all
- out_weight: bfloat16 [1024, 3584], P('tensor'), may hold values from -0.53125 to 0.53125
- post_gain: float32 [3584], replicated, may hold values from 0.1 to 1.9
- ffn_gain: float32 [3584], replicated, may hold values from 0.1 to 1.9
- gate_weight: bfloat16 [3584, 3584], P('ctx', 'tensor'), may hold values from -0.09375 to 0.09375
- up_weight: bfloat16 [3584, 3584], P('ctx', 'tensor'), may hold values from -0.09375 to 0.09375
Outputs:
- mixed_stream: bfloat16 [2048, 3584], P(('dp', 'ctx', 'tensor')), parts along dimension 0
- ffn_hidden: bfloat16 [2048, 3584], P(('dp', 'ctx'), 'tensor'), parts along dimension 0
There are 2 independent parts, one for each index of `dp`. A program takes and returns all parts, laid end to end along the dimension named above; an argument that names none is the same for every part. Nothing has to cross between parts.
Inputs may be any that keep to these rules, and one draw needn't show every extreme that they name: `doc_blocks`: the lengths, in blocks of 32 positions, of the 6 documents packed in order into the sequence; they sum to 32, and the longest has exactly 16 blocks.
All inputs are finite; a program needn't handle non-finite values.
Results may differ from a plain program's by a relative error of at most 0.025.
Values may be sent and summed in bfloat16 or wider, within the bound.
A program may use at most 64 MiB of HBM per device.

v0:
```python
import jax
import jax.numpy as jnp
from jax import lax
from jax.sharding import PartitionSpec as P

BLOCK = 32
SOFT_CAP = 50.0
NORM_EPS = 1e-06
ROPE_BASE = 10000.0


def partner_2(value, axis, apart):
    mask = 2**apart
    pairs = [(source, source ^ mask) for source in range(lax.axis_size(axis))]
    return lax.ppermute(value, axis, pairs)


def rope_angles(positions, head_size):
    halfway = head_size // 2
    frequency = ROPE_BASE ** (-(jnp.arange(halfway, dtype=jnp.float32) * 2.0) / head_size)
    angles = positions.astype(jnp.float32)[:, None] * frequency[None, :]
    return (jnp.cos(angles), jnp.sin(angles))


def rotate(heads_in, cosine, sine_value, head_size):
    rows_here = heads_in.shape[0]
    reshaped = heads_in.astype(jnp.float32).reshape(rows_here, -1, head_size)
    leading = reshaped[:, :, : head_size // 2]
    trailing = reshaped[:, :, head_size // 2 :]
    cos_wide = cosine[:, None, :]
    sin_wide = sine_value[:, None, :]
    turned = jnp.concatenate(
        [leading * cos_wide - trailing * sin_wide, trailing * cos_wide + leading * sin_wide], axis=2
    )
    return turned.reshape(rows_here, -1).astype(jnp.bfloat16)


def doc_of(positions, doc_blocks):
    doc_ends = jnp.cumsum(doc_blocks)
    passed = positions[:, None] // BLOCK >= doc_ends[None, :]
    return jnp.sum(passed.astype(jnp.int32), axis=1)


def rms_scale(values):
    return values * lax.rsqrt(jnp.mean(values * values, axis=-1, keepdims=True) + NORM_EPS)


def gelu_gate(gate_sum, up_sum):
    return (jax.nn.gelu(gate_sum, approximate=True) * up_sum).astype(jnp.bfloat16)


def attend(query_rows, query_pos, query_doc, key_rows, value_rows, key_pos, key_doc, score_scale):
    scores = (
        lax.dot_general(
            query_rows, key_rows, (((1,), (1,)), ((), ())), preferred_element_type=jnp.float32
        )
        * score_scale
    )
    capped = SOFT_CAP * jnp.tanh(scores / SOFT_CAP)
    visible = (key_pos[None, :] <= query_pos[:, None]) & (key_doc[None, :] == query_doc[:, None])
    weights = jnp.where(visible, jnp.exp(capped), 0.0).astype(jnp.bfloat16)
    numerator = jnp.dot(weights, value_rows, preferred_element_type=jnp.float32)
    denominator = jnp.sum(weights.astype(jnp.float32), axis=1)
    return (numerator, denominator)


def join_halves(own_part, other_part, own_first):
    return jnp.where(
        own_first,
        jnp.concatenate([own_part, other_part], axis=2),
        jnp.concatenate([other_part, own_part], axis=2),
    )


def per_device(
    residual,
    queries,
    key_heads,
    value_heads,
    doc_blocks,
    out_weight,
    post_gain,
    ffn_gain,
    gate_weight,
    up_weight,
):
    tok_rows = queries.shape[0]
    head_size = queries.shape[1]
    score_scale = head_size ** (-0.5)
    query_pos = lax.axis_index("ctx") * tok_rows + jnp.arange(tok_rows, dtype=jnp.int32)
    query_doc = doc_of(query_pos, doc_blocks)
    cosine, sine_value = rope_angles(query_pos, head_size)
    query_rot = rotate(queries, cosine, sine_value, head_size)
    stacked = jnp.stack([key_heads, value_heads])
    own_first = lax.axis_index("tensor") % 2 == 0
    partner = partner_2(stacked, "tensor", 0)
    joined = join_halves(stacked, partner, own_first)
    key_rot = rotate(joined[0], cosine, sine_value, head_size)
    shard_pair = (
        lax.all_gather(key_rot, "ctx", axis=0, tiled=True),
        lax.all_gather(joined[1], "ctx", axis=0, tiled=True),
    )
    key_pos = jnp.arange(shard_pair[0].shape[0], dtype=jnp.int32)
    numerator, denominator = attend(
        query_rot,
        query_pos,
        query_doc,
        shard_pair[0],
        shard_pair[1],
        key_pos,
        doc_of(key_pos, doc_blocks),
        score_scale,
    )
    attended = (numerator / denominator[:, None]).astype(jnp.bfloat16)
    attn_rows = lax.psum_scatter(
        jnp.dot(attended, out_weight, preferred_element_type=jnp.float32).astype(jnp.bfloat16),
        "tensor",
        scatter_dimension=0,
        tiled=True,
    ).astype(jnp.float32)
    mixed_stream = (residual.astype(jnp.float32) + rms_scale(attn_rows) * post_gain).astype(
        jnp.bfloat16
    )
    ffn_input = (rms_scale(mixed_stream.astype(jnp.float32)) * ffn_gain).astype(jnp.bfloat16)
    gathered_rows = lax.all_gather(ffn_input, "tensor", axis=0, tiled=True)
    shard_pair = (
        lax.all_gather(gate_weight, "ctx", axis=0, tiled=True),
        lax.all_gather(up_weight, "ctx", axis=0, tiled=True),
    )
    gate_part = jnp.dot(gathered_rows, shard_pair[0], preferred_element_type=jnp.float32)
    up_part = jnp.dot(gathered_rows, shard_pair[1], preferred_element_type=jnp.float32)
    ffn_hidden = gelu_gate(gate_part, up_part)
    return (mixed_stream, ffn_hidden)


def solution(mesh):
    in_specs = (
        P(("dp", "ctx", "tensor"), None),
        P(("dp", "ctx"), "tensor"),
        P(("dp", "ctx"), "tensor"),
        P(("dp", "ctx"), "tensor"),
        P("dp"),
        P("tensor", None),
        P(),
        P(),
        P("ctx", "tensor"),
        P("ctx", "tensor"),
    )
    out_specs = (P(("dp", "ctx", "tensor"), None), P(("dp", "ctx"), "tensor"))
    return jax.shard_map(
        per_device, mesh=mesh, in_specs=in_specs, out_specs=out_specs, check_vma=False
    )
```

profile of v0, /device:TPU:0, one launch (start us, length us, event | category | flops | bytes accessed | tf_op | source)
XLA Modules:
  0.0 227.5 jit_solution(10332107046243191215)
XLA Ops:
  7.2 0.0 copy-start
  7.2 0.0 reduce-scatter.2.cloned.1.call-start
  7.2 1.0 pad_maximum_fusion
  8.2 3.1 %collective-permute-start = (bf16[2,256,128]{2,1,0:T(8,128)(2,1)S(1)}, bf16[2,256,128]{2,1,0:T(8,128)(2,1)S(1)}, u32[]{:S(2)}, u32[]{:S(2)}) collective-permute-start(bf16[2,256,128]{2,1,0:T(8,128)(2,1)S(1)} %pad_maximum_fusion), channel_id=1, source_target_pairs={{0,1},{1,0},{2,3},{3,2},{4,5},{5,4},{6,7},{7,6},{8,9},{9,8},{10,11... | collective-permute-start | bytes 393224 | tf_op jit(solution)/shard_map/ppermute | solution.py:15
  11.4 0.9 bitcast_convert_fusion
  12.3 0.8 reduce-window.8
  13.1 0.1 convert_reduce_fusion.2
  13.2 0.1 convert_reduce_fusion.1
  13.3 1.5 collective-permute-done
  14.9 1.0 maximum_select_fusion
  15.9 0.6 fusion.34
  16.5 7.3 %all-gather = bf16[1024,1,256]{2,0,1:T(8,128)(2,1)S(1)} all-gather(bf16[256,1,256]{2,0,1:T(8,128)(2,1)S(1)} %pad_maximum_fusion.1), channel_id=2, replica_groups=mesh['dp'=2,'ctx'=4,'tensor'=4] {'ctx'}, dimensions={0}, use_global_device_ids=true | all-gather | bytes 655360 | tf_op jit(solution)/shard_map/all_gather | solution.py:100
  23.9 7.3 %all-gather.1 = bf16[1,1024,256]{2,1,0:T(8,128)(2,1)S(1)} all-gather(bf16[1,256,256]{2,1,0:T(8,128)(2,1)S(1)} %get-tuple-element.8), channel_id=3, replica_groups=mesh['dp'=2,'ctx'=4,'tensor'=4] {'ctx'}, dimensions={1}, use_global_device_ids=true | all-gather | bytes 655360 | tf_op jit(solution)/shard_map/all_gather | solution.py:101
  31.1 0.7 convert_reduce_fusion
  31.8 0.0 copy-done
  31.8 2.4 %convolution_convert_fusion = bf16[256,3584]{1,0:T(8,128)(2,1)} fusion(bf16[256,3584]{1,0:T(8,128)(2,1)S(1)} %copy-done, bf16[256,1024]{1,0:T(8,128)(2,1)S(1)} %get-tuple-element.13, bf16[1,1024,256]{2,1,0:T(8,128)(2,1)S(1)} %all-gather.1, f32[256]{0:T(256)S(1)} %get-tuple-element.12), kind=kOutput, calls=%fused_computation | convolution fusion | flops 605028352 | bytes 4719616 | tf_op jit(solution)/shard_map/dot_general | solution.py:116
  34.2 0.0 copy-start.2
  34.2 0.0 copy-start.3
  34.2 0.0 copy-start.4
  34.2 0.0 reduce-scatter.2.cloned.1.call-update
  34.2 0.0 all-gather.6.cloned.1.call-start
  34.3 40.2 %reduce-scatter.2.cloned.1.call-done = bf16[64,3584]{1,0:T(8,128)(2,1)} async-done(((bf16[256,3584]{1,0:T(8,128)(2,1)}), bf16[64,3584]{1,0:T(8,128)(2,1)}) %reduce-scatter.2.cloned.1.call-update) | async-done | bytes 458768 | tf_op jit(solution)/shard_map/reduce_scatter | solution.py:115
  74.5 1.2 fusion.8
  75.7 0.0 copy-done.2
  75.7 0.0 copy-done.3
  75.7 1.4 fusion.12
  77.1 0.0 copy-start.1
  77.2 0.0 copy-done.4
  77.2 0.9 fusion.14
  78.1 0.0 all-gather.6.cloned.1.call-update
  78.1 0.0 all-gather.8.cloned.1.call-start
  78.2 0.7 all-gather.8.cloned.1.call-update
  78.9 0.0 all-gather.10.cloned.1.call-start
  78.9 0.5 all-gather.10.cloned.1.call-update
  79.5 0.0 copy-done.1
  79.5 39.2 %all-gather.6.cloned.1.call-done = bf16[256,3584]{1,0:T(8,128)(2,1)} async-done(((bf16[64,3584]{1,0:T(8,128)(2,1)}), bf16[256,3584]{1,0:T(8,128)(2,1)}) %all-gather.6.cloned.1.call-update) | async-done | bytes 1835024 | tf_op jit(solution)/shard_map/all_gather | solution.py:125
  118.7 47.5 %all-gather.8.cloned.1.call-done = bf16[3584,896]{1,0:T(8,128)(2,1)} async-done(((bf16[896,896]{1,0:T(8,128)(2,1)}), bf16[3584,896]{1,0:T(8,128)(2,1)}) %all-gather.8.cloned.1.call-update) | async-done | bytes 6422544 | tf_op jit(solution)/shard_map/all_gather | solution.py:127
  166.2 5.5 %fusion.52 = f32[256,896]{1,0:T(8,128)S(1)} fusion(bf16[256,3584]{1,0:T(8,128)(2,1)} %all-gather.6.cloned.1.call-done, bf16[3584,896]{1,0:T(8,128)(2,1)} %all-gather.8.cloned.1.call-done), kind=kOutput, calls=%fused_computation.83 | convolution fusion | flops 1644167168 | bytes 9175040 | tf_op jit(solution)/shard_map/dot_general | solution.py:130
  171.6 43.1 %all-gather.10.cloned.1.call-done = bf16[3584,896]{1,0:T(8,128)(2,1)} async-done(((bf16[896,896]{1,0:T(8,128)(2,1)}), bf16[3584,896]{1,0:T(8,128)(2,1)}) %all-gather.10.cloned.1.call-update) | async-done | bytes 6422544 | tf_op jit(solution)/shard_map/all_gather | solution.py:128
  214.7 6.3 %fusion.5 = bf16[256,896]{1,0:T(8,128)(2,1)} fusion(bf16[256,3584]{1,0:T(8,128)(2,1)} %all-gather.6.cloned.1.call-done, bf16[3584,896]{1,0:T(8,128)(2,1)} %all-gather.10.cloned.1.call-done, f32[256,896]{1,0:T(8,128)S(1)} %fusion.52), kind=kOutput, calls=%fused_computation.9 | convolution fusion | flops 1646460928 | bytes 9633792 | tf_op jit(solution)/shard_map/dot_general | solution.py:131
  (8 shorter events, 0.1 us)
Async XLA Ops:
  7.2 24.7 %copy-start = (bf16[256,3584]{1,0:T(8,128)(2,1)S(1)}, bf16[256,3584]{1,0:T(8,128)(2,1)}, u32[]{:S(2)}) copy-start(bf16[256,3584]{1,0:T(8,128)(2,1)} %param.15) | copy-start | bytes 5505028
  7.2 67.3 %reduce-scatter.2.cloned.1.call-start = ((), (), s32[]{:S(2)}) async-start(), calls=%async_computation.1 | async-start | bytes 2293760 | tf_op jit(solution)/shard_map/reduce_scatter | solution.py:115
  8.2 6.6 %collective-permute-start = (bf16[2,256,128]{2,1,0:T(8,128)(2,1)S(1)}, bf16[2,256,128]{2,1,0:T(8,128)(2,1)S(1)}, u32[]{:S(2)}, u32[]{:S(2)}) collective-permute-start(bf16[2,256,128]{2,1,0:T(8,128)(2,1)S(1)} %pad_maximum_fusion), channel_id=1, source_target_pairs={{0,1},{1,0},{2,3},{3,2},{4,5},{5,4},{6,7},{7,6},{8,9},{9,8},{10,11... | collective-permute-start | bytes 393224 | tf_op jit(solution)/shard_map/ppermute | solution.py:15
  34.2 41.5 %copy-start.2 = (bf16[64,3584]{1,0:T(8,128)(2,1)S(1)}, bf16[64,3584]{1,0:T(8,128)(2,1)}, u32[]{:S(2)}) copy-start(bf16[64,3584]{1,0:T(8,128)(2,1)} %param.10) | copy-start | bytes 1376260
  34.2 41.5 %copy-start.3 = (f32[3584]{0:T(1024)S(1)}, f32[3584]{0:T(1024)}, u32[]{:S(2)}) copy-start(f32[3584]{0:T(1024)} %param.16) | copy-start | bytes 43012
  34.2 43.0 %copy-start.4 = (f32[3584]{0:T(1024)S(1)}, f32[3584]{0:T(1024)}, u32[]{:S(2)}) copy-start(f32[3584]{0:T(1024)} %param.17) | copy-start | bytes 43012
  34.2 84.4 %all-gather.6.cloned.1.call-start = ((), (), s32[]{:S(2)}) async-start(), calls=%async_computation.2 | async-start | bytes 2293760 | tf_op jit(solution)/shard_map/all_gather | solution.py:125
  77.1 2.3 %copy-start.1 = (bf16[64,3584]{1,0:T(8,128)(2,1)}, bf16[64,3584]{1,0:T(8,128)(2,1)S(1)}, u32[]{:S(2)}) copy-start(bf16[64,3584]{1,0:T(8,128)(2,1)S(1)} %get-tuple-element.3) | copy-start | bytes 1376260
  78.1 88.0 %all-gather.8.cloned.1.call-start = ((), (), s32[]{:S(2)}) async-start(), calls=%async_computation.3 | async-start | bytes 8028160 | tf_op jit(solution)/shard_map/all_gather | solution.py:127
  78.9 135.9 %all-gather.10.cloned.1.call-start = ((), (), s32[]{:S(2)}) async-start(), calls=%async_computation.4 | async-start | bytes 8028160 | tf_op jit(solution)/shard_map/all_gather | solution.py:128
Sparse Core Ops, SparseCore 0:
  34.4 40.0 reduce-scatter.1
  78.3 40.3 all-gather.5
  120.2 45.9 all-gather.7
  167.6 47.0 all-gather.9
where the time goes:
time: 228 us
  waiting for transfers between devices  173 us (76%)
  matrix products  14.8 us (6%)
  blocking collectives  14.6 us (6%)
  between operations  13.9 us (6%)
  other arithmetic  8.2 us (4%)
  starting transfers between devices  3.28 us (1%)
    all_gather x1, waiting for transfers between devices, per_device(): lax.all_gather(gate_weight, 'ctx', axis=0, tiled=True)  47.5 us
    all_gather x1, waiting for transfers between devices, per_device(): lax.all_gather(up_weight, 'ctx', axis=0, tiled=True)  43.1 us
    reduce_scatter x1, waiting for transfers between devices, per_device(): lax.psum_scatter(jnp.dot(attended, out_weight, preferred_element_type=jnp...  40.2 us
    all_gather x1, waiting for transfers between devices, per_device(): gathered_rows = lax.all_gather(ffn_input, 'tensor', axis=0, tiled=True)  39.2 us
    all_gather x1, blocking collectives, per_device(): lax.all_gather(key_rot, 'ctx', axis=0, tiled=True)  7.34 us
    all_gather x1, blocking collectives, per_device(): lax.all_gather(joined[1], 'ctx', axis=0, tiled=True)  7.26 us
    dot_general x1, matrix products, per_device(): jnp.dot(gathered_rows, shard_pair[1], preferred_element_type=jnp.float32)  6.25 us
    dot_general x1, matrix products, per_device(): jnp.dot(gathered_rows, shard_pair[0], preferred_element_type=jnp.float32)  5.45 us
  transfers between devices with their start and end apart: 5, of which 5 were waited for; matrix products, arithmetic and copies ran while one was open for 3% of the time, Pallas kernels for 0%

commit v1 on v0

--- a/solution.py
+++ b/solution.py
@@ -122,7 +122,20 @@
         jnp.bfloat16
     )
     ffn_input = (rms_scale(mixed_stream.astype(jnp.float32)) * ffn_gain).astype(jnp.bfloat16)
-    gathered_rows = lax.all_gather(ffn_input, "tensor", axis=0, tiled=True)
+
+    def advance_the_terms(net_axis, sample):
+        chips = lax.axis_size(net_axis)
+        b_next = sorted(((j, (j + 1) % chips) for j in range(chips)))
+        current_block = sample
+        log = [current_block]
+        for pp in tuple(range(1, chips)):
+            current_block = lax.ppermute(current_block, net_axis, b_next)
+            log.insert(0, current_block)
+        e_now = jnp.concatenate(log, axis=0)
+        now = lax.axis_index(net_axis)
+        return jnp.roll(e_now, shift=(now + 1) * sample.shape[0], axis=0)
+
+    gathered_rows = advance_the_terms("tensor", ffn_input)
     shard_pair = (
         lax.all_gather(gate_weight, "ctx", axis=0, tiled=True),
         lax.all_gather(up_weight, "ctx", axis=0, tiled=True),

time: 228 us -> 147 us (0.64)
  waiting for transfers between devices: 173 us -> 81.7 us
  local copies, waits for them, and re-layouts: 0.03 us -> 6.97 us
    all_gather x1, waiting for transfers between devices: 47.5 us -> 2.09 us  [per_device(): lax.all_gather(gate_weight, 'ctx', axis=0, tiled=True)]
    all_gather x1, waiting for transfers between devices: 43.1 us -> 0.01 us  [per_device(): lax.all_gather(up_weight, 'ctx', axis=0, tiled=True)]
    all_gather x1 -> x0, waiting for transfers between devices: 39.2 us -> none  [per_device(): gathered_rows = lax.all_gather(ffn_input, 'tensor', axis=0, tiled=True)]
    ppermute x0 -> x3, waiting for transfers between devices: none -> 38 us  [advance_the_terms(): current_block = lax.ppermute(current_block, net_axis, b_next)]
    unnamed x10 -> x16, local copies, waits for them, and re-layouts: 0.03 us -> 6.97 us
  transfers between devices with their start and end apart: 5 -> 7, of which waited for: 5 -> 6; matrix products, arithmetic and copies ran while one was open for 3% -> 13% of each run, Pallas kernels for 0% -> 0%
where the time goes in v1:
time: 147 us
  waiting for transfers between devices  81.7 us (56%)
  between operations  15.6 us (11%)
  matrix products  14.9 us (10%)
  blocking collectives  14.6 us (10%)
  other arithmetic  9.35 us (6%)
  local copies, waits for them, and re-layouts  6.97 us (5%)
  starting transfers between devices  3.77 us (3%)
    reduce_scatter x1, waiting for transfers between devices, per_device(): lax.psum_scatter(jnp.dot(attended, out_weight, preferred_element_type=jnp...  39.1 us
    ppermute x3, waiting for transfers between devices, advance_the_terms(): current_block = lax.ppermute(current_block, net_axis, b_next)  38 us
    all_gather x1, blocking collectives, per_device(): lax.all_gather(key_rot, 'ctx', axis=0, tiled=True)  7.34 us
    all_gather x1, blocking collectives, per_device(): lax.all_gather(joined[1], 'ctx', axis=0, tiled=True)  7.26 us
    unnamed x16, local copies, waits for them, and re-layouts  6.97 us
    dot_general x1, matrix products, per_device(): jnp.dot(gathered_rows, shard_pair[0], preferred_element_type=jnp.float32)  6.39 us
    dot_general x1, matrix products, per_device(): jnp.dot(gathered_rows, shard_pair[1], preferred_element_type=jnp.float32)  5.45 us
    ppermute x1, starting transfers between devices, partner_2(): return lax.ppermute(value, axis, pairs)  3.12 us
  transfers between devices with their start and end apart: 7, of which 6 were waited for; matrix products, arithmetic and copies ran while one was open for 13% of the time, Pallas kernels for 0%

profile of v1, /device:TPU:0, one launch (start us, length us, event | category | flops | bytes accessed | tf_op | source)
XLA Modules:
  0.0 146.9 jit_solution(6752595434864188039)
XLA Ops:
  8.0 0.0 copy-start
  8.0 0.0 reduce-scatter.2.cloned.1.call-start
  8.1 1.0 pad_maximum_fusion
  9.1 3.1 %collective-permute-start = (bf16[2,256,128]{2,1,0:T(8,128)(2,1)S(1)}, bf16[2,256,128]{2,1,0:T(8,128)(2,1)S(1)}, u32[]{:S(2)}, u32[]{:S(2)}) collective-permute-start(bf16[2,256,128]{2,1,0:T(8,128)(2,1)S(1)} %pad_maximum_fusion), channel_id=1, source_target_pairs={{0,1},{1,0},{2,3},{3,2},{4,5},{5,4},{6,7},{7,6},{8,9},{9,8},{10,11... | collective-permute-start | bytes 393224 | tf_op jit(solution)/shard_map/ppermute | solution.py:15
  12.2 0.9 bitcast_convert_fusion
  13.1 0.8 reduce-window.8
  14.0 0.1 convert_reduce_fusion.2
  14.1 0.1 convert_reduce_fusion.1
  14.2 1.5 %collective-permute-done = bf16[2,256,128]{2,1,0:T(8,128)(2,1)S(1)} collective-permute-done((bf16[2,256,128]{2,1,0:T(8,128)(2,1)S(1)}, bf16[2,256,128]{2,1,0:T(8,128)(2,1)S(1)}, u32[]{:S(2)}, u32[]{:S(2)}) %collective-permute-start) | collective-permute-done | bytes 131104 | tf_op jit(solution)/shard_map/ppermute | solution.py:15
  15.7 1.0 maximum_select_fusion
  16.7 0.6 fusion.45
  17.4 7.3 %all-gather = bf16[1024,1,256]{2,0,1:T(8,128)(2,1)S(1)} all-gather(bf16[256,1,256]{2,0,1:T(8,128)(2,1)S(1)} %pad_maximum_fusion.1), channel_id=2, replica_groups=mesh['dp'=2,'ctx'=4,'tensor'=4] {'ctx'}, dimensions={0}, use_global_device_ids=true | all-gather | bytes 655360 | tf_op jit(solution)/shard_map/all_gather | solution.py:100
  24.7 7.3 %all-gather.1 = bf16[1,1024,256]{2,1,0:T(8,128)(2,1)S(1)} all-gather(bf16[1,256,256]{2,1,0:T(8,128)(2,1)S(1)} %get-tuple-element.8), channel_id=3, replica_groups=mesh['dp'=2,'ctx'=4,'tensor'=4] {'ctx'}, dimensions={1}, use_global_device_ids=true | all-gather | bytes 655360 | tf_op jit(solution)/shard_map/all_gather | solution.py:101
  32.0 0.7 convert_reduce_fusion
  32.7 0.0 copy-done
  32.7 2.4 %convolution_convert_fusion = bf16[256,3584]{1,0:T(8,128)(2,1)} fusion(bf16[256,3584]{1,0:T(8,128)(2,1)S(1)} %copy-done, bf16[256,1024]{1,0:T(8,128)(2,1)S(1)} %get-tuple-element.13, bf16[1,1024,256]{2,1,0:T(8,128)(2,1)S(1)} %all-gather.1, f32[256]{0:T(256)S(1)} %get-tuple-element.12), kind=kOutput, calls=%fused_computation | convolution fusion | flops 605028352 | bytes 4719616 | tf_op jit(solution)/shard_map/dot_general | solution.py:116
  35.0 0.0 copy-start.2
  35.0 0.0 copy-start.4
  35.0 0.0 copy-start.3
  35.0 0.0 reduce-scatter.2.cloned.1.call-update
  35.1 0.0 all-gather.7.cloned.1.call-start
  35.1 0.5 all-gather.7.cloned.1.call-update
  35.6 0.0 all-gather.5.cloned.1.call-start
  35.7 0.5 all-gather.5.cloned.1.call-update
  36.2 39.1 %reduce-scatter.2.cloned.1.call-done = bf16[64,3584]{1,0:T(8,128)(2,1)} async-done(((bf16[256,3584]{1,0:T(8,128)(2,1)}), bf16[64,3584]{1,0:T(8,128)(2,1)}) %reduce-scatter.2.cloned.1.call-update) | async-done | bytes 458768 | tf_op jit(solution)/shard_map/reduce_scatter | solution.py:115
  75.3 1.2 fusion.11
  76.6 0.0 copy-done.2
  76.6 0.0 copy-done.4
  76.6 1.4 fusion.15
  78.0 0.0 copy-start.1
  78.0 0.0 copy-done.3
  78.0 0.2 fusion.17
  78.2 0.5 collective-permute-start.1
  78.7 13.2 %collective-permute-done.1 = bf16[64,3584]{1,0:T(8,128)(2,1)S(1)} collective-permute-done((bf16[64,3584]{1,0:T(8,128)(2,1)S(1)}, bf16[64,3584]{1,0:T(8,128)(2,1)S(1)}, u32[]{:S(2)}, u32[]{:S(2)}) %collective-permute-start.1) | collective-permute-done | bytes 458784 | tf_op jit(solution)/shard_map/ppermute | solution.py:132
  91.9 0.0 collective-permute-start.2
  91.9 12.8 %collective-permute-done.2 = bf16[64,3584]{1,0:T(8,128)(2,1)S(1)} collective-permute-done((bf16[64,3584]{1,0:T(8,128)(2,1)S(1)}, bf16[64,3584]{1,0:T(8,128)(2,1)S(1)}, u32[]{:S(2)}, u32[]{:S(2)}) %collective-permute-start.2) | collective-permute-done | bytes 458784 | tf_op jit(solution)/shard_map/ppermute | solution.py:132
  104.7 0.0 collective-permute-start.3
  104.7 12.0 %collective-permute-done.3 = bf16[64,3584]{1,0:T(8,128)(2,1)} collective-permute-done((bf16[64,3584]{1,0:T(8,128)(2,1)S(1)}, bf16[64,3584]{1,0:T(8,128)(2,1)}, u32[]{:S(2)}, u32[]{:S(2)}) %collective-permute-start.3) | collective-permute-done | bytes 458784 | tf_op jit(solution)/shard_map/ppermute | solution.py:132
  116.7 1.8 %constant_dynamic-update-slice_fusion.7 = bf16[512,3584]{1,0:T(8,128)(2,1)} fusion(bf16[64,3584]{1,0:T(8,128)(2,1)} %collective-permute-done.3), kind=kLoop, calls=%fused_computation.75 | loop fusion | bytes 917504
  118.6 0.8 constant_dynamic-update-slice_fusion.6
  119.4 0.8 constant_dynamic-update-slice_fusion.5
  120.2 0.9 constant_dynamic-update-slice_fusion.4
  121.1 1.8 %constant_dynamic-update-slice_fusion.3 = bf16[512,3584]{1,0:T(8,128)(2,1)} fusion(bf16[512,3584]{1,0:T(8,128)(2,1)} %constant_dynamic-update-slice_fusion.4, bf16[64,3584]{1,0:T(8,128)(2,1)} %collective-permute-done.3), kind=kLoop, calls=%fused_computation.71 | loop fusion | bytes 917504
  123.0 0.8 constant_dynamic-update-slice_fusion.2
  123.8 0.8 constant_dynamic-update-slice_fusion.1
  124.6 0.0 copy-done.1
  124.6 1.0 constant_dynamic-update-slice_fusion
  125.6 0.0 all-gather.7.cloned.1.call-done
  125.6 5.5 %fusion = f32[256,896]{1,0:T(8,128)S(1)} fusion(bf16[3584,896]{1,0:T(8,128)(2,1)} %all-gather.7.cloned.1.call-done, bf16[512,3584]{1,0:T(8,128)(2,1)} %constant_dynamic-update-slice_fusion, s32[]{:T(128)S(6)} %select_n.58), kind=kOutput, calls=%fused_computation.1 | convolution fusion | flops 1644167168 | bytes 9175044 | tf_op jit(solution)/shard_map/dot_general | solution.py:144
  131.0 2.1 %all-gather.5.cloned.1.call-done = bf16[3584,896]{1,0:T(8,128)(2,1)} async-done(((bf16[896,896]{1,0:T(8,128)(2,1)}), bf16[3584,896]{1,0:T(8,128)(2,1)}) %all-gather.5.cloned.1.call-update) | async-done | bytes 6422544 | tf_op jit(solution)/shard_map/all_gather | solution.py:140
  133.1 6.4 %fusion.30 = bf16[256,896]{1,0:T(8,128)(2,1)} fusion(f32[256,896]{1,0:T(8,128)S(1)} %fusion, bf16[3584,896]{1,0:T(8,128)(2,1)} %all-gather.5.cloned.1.call-done, bf16[512,3584]{1,0:T(8,128)(2,1)} %constant_dynamic-update-slice_fusion, s32[]{:T(128)S(6)} %select_n.58), kind=kOutput, calls=%fused_computation.36 | convolution fusion | flops 1646460928 | bytes 9633796 | tf_op jit(solution)/shard_map/dot_general | solution.py:143
  (8 shorter events, 0.1 us)
Async XLA Ops:
  8.0 24.7 %copy-start = (bf16[256,3584]{1,0:T(8,128)(2,1)S(1)}, bf16[256,3584]{1,0:T(8,128)(2,1)}, u32[]{:S(2)}) copy-start(bf16[256,3584]{1,0:T(8,128)(2,1)} %param.15) | copy-start | bytes 5505028
  8.0 67.3 %reduce-scatter.2.cloned.1.call-start = ((), (), s32[]{:S(2)}) async-start(), calls=%async_computation.1 | async-start | bytes 2293760 | tf_op jit(solution)/shard_map/reduce_scatter | solution.py:115
  9.1 6.6 %collective-permute-start = (bf16[2,256,128]{2,1,0:T(8,128)(2,1)S(1)}, bf16[2,256,128]{2,1,0:T(8,128)(2,1)S(1)}, u32[]{:S(2)}, u32[]{:S(2)}) collective-permute-start(bf16[2,256,128]{2,1,0:T(8,128)(2,1)S(1)} %pad_maximum_fusion), channel_id=1, source_target_pairs={{0,1},{1,0},{2,3},{3,2},{4,5},{5,4},{6,7},{7,6},{8,9},{9,8},{10,11... | collective-permute-start | bytes 393224 | tf_op jit(solution)/shard_map/ppermute | solution.py:15
  35.0 41.5 %copy-start.2 = (bf16[64,3584]{1,0:T(8,128)(2,1)S(1)}, bf16[64,3584]{1,0:T(8,128)(2,1)}, u32[]{:S(2)}) copy-start(bf16[64,3584]{1,0:T(8,128)(2,1)} %param.10) | copy-start | bytes 1376260
  35.0 41.5 %copy-start.4 = (f32[3584]{0:T(1024)S(1)}, f32[3584]{0:T(1024)}, u32[]{:S(2)}) copy-start(f32[3584]{0:T(1024)} %param.16) | copy-start | bytes 43012
  35.0 43.0 %copy-start.3 = (f32[3584]{0:T(1024)S(1)}, f32[3584]{0:T(1024)}, u32[]{:S(2)}) copy-start(f32[3584]{0:T(1024)} %param.17) | copy-start | bytes 43012
  35.1 90.5 %all-gather.7.cloned.1.call-start = ((), (), s32[]{:S(2)}) async-start(), calls=%async_computation.3 | async-start | bytes 8028160 | tf_op jit(solution)/shard_map/all_gather | solution.py:141
  35.6 97.5 %all-gather.5.cloned.1.call-start = ((), (), s32[]{:S(2)}) async-start(), calls=%async_computation.2 | async-start | bytes 8028160 | tf_op jit(solution)/shard_map/all_gather | solution.py:140
  78.0 46.6 %copy-start.1 = (bf16[64,3584]{1,0:T(8,128)(2,1)}, bf16[64,3584]{1,0:T(8,128)(2,1)S(1)}, u32[]{:S(2)}) copy-start(bf16[64,3584]{1,0:T(8,128)(2,1)S(1)} %get-tuple-element.3) | copy-start | bytes 1376260
  78.2 13.7 %collective-permute-start.1 = (bf16[64,3584]{1,0:T(8,128)(2,1)S(1)}, bf16[64,3584]{1,0:T(8,128)(2,1)S(1)}, u32[]{:S(2)}, u32[]{:S(2)}) collective-permute-start(bf16[64,3584]{1,0:T(8,128)(2,1)S(1)} %fusion.17), channel_id=1, source_target_pairs={{0,1},{1,2},{2,3},{3,0},{4,5},{5,6},{6,7},{7,4},{8,9},{9,10},{10,1... | collective-permute-start | bytes 1376264 | tf_op jit(solution)/shard_map/ppermute | solution.py:132
  91.9 12.8 %collective-permute-start.2 = (bf16[64,3584]{1,0:T(8,128)(2,1)S(1)}, bf16[64,3584]{1,0:T(8,128)(2,1)S(1)}, u32[]{:S(2)}, u32[]{:S(2)}) collective-permute-start(bf16[64,3584]{1,0:T(8,128)(2,1)S(1)} %collective-permute-done.1), channel_id=1, source_target_pairs={{0,1},{1,2},{2,3},{3,0},{4,5},{5,6},{6,7},{7,4},{8,9},{9,10},{10,1... | collective-permute-start | bytes 1376264 | tf_op jit(solution)/shard_map/ppermute | solution.py:132
  104.7 12.0 %collective-permute-start.3 = (bf16[64,3584]{1,0:T(8,128)(2,1)S(1)}, bf16[64,3584]{1,0:T(8,128)(2,1)}, u32[]{:S(2)}, u32[]{:S(2)}) collective-permute-start(bf16[64,3584]{1,0:T(8,128)(2,1)S(1)} %collective-permute-done.2), channel_id=1, source_target_pairs={{0,1},{1,2},{2,3},{3,0},{4,5},{5,6},{6,7},{7,4},{8,9},{9,10},{10,1... | collective-permute-start | bytes 1376264 | tf_op jit(solution)/shard_map/ppermute | solution.py:132
Sparse Core Ops, SparseCore 0:
  35.2 40.0 reduce-scatter.1
Sparse Core Ops, SparseCore 1:
  37.1 47.5 all-gather.6
  86.1 46.9 all-gather.4
